TPU v7x, 32 devices: a whole 2x2x4 slice. The times are simulated.
32 devices in a mesh: real: 2 (over x), tile: 16 (over z, y, core).
Axes of the slice: x: 2, y: 2, z: 4, core: 2. Of those that a mesh axis runs over, the one named last changes fastest.
Arguments:
- positions: float32 [6, 8192], P('real', 'tile'), parts along dimension 0, may hold values from -1.5 to 125.5, as said below
- residual: float32 [6, 8192], P('real', 'tile'), parts along dimension 0, may hold values from -24 to 24
- iterate: float32 [6, 8192], P('real', 'tile'), parts along dimension 0, may hold values from -6 to 6
Outputs:
- new_iterate: float32 [6, 8192], P('real', 'tile'), parts along dimension 0
- new_residual: float32 [6, 8192], P('real', 'tile'), parts along dimension 0
- new_direction: float32 [6, 8192], P('real', 'tile'), parts along dimension 0
There are 2 independent parts, one for each index of `real`. A program takes and returns all parts, laid end to end along the dimension named above; each array names one. Nothing has to cross between parts.
Inputs may be any that keep to these rules, and one draw needn't show every extreme that they name: `positions`: distinct blobs are at least 1 apart.
All inputs are finite; a program needn't handle non-finite values.
Results may differ from a plain program's by a relative error of at most 0.0003.
Values sent between devices are 32-bit elements; how exact they have to be, the bound alone decides.
A program may use at most 64 MiB of HBM per device.

v0:
```python
import jax
import jax.numpy as jnp
from jax import lax
from jax.sharding import PartitionSpec as P


def pair_terms(row_pos, col_pos):
    separation = row_pos[:, :, None] - col_pos[:, None, :]
    squared = jnp.sum(separation * separation, axis=0)
    radius = jnp.sqrt(squared)
    inverse = 1.0 / jnp.maximum(radius, 0.5)
    inverse_sq = inverse * inverse
    far_scalar = 0.75 * inverse * (1.0 + 2.0 / 3.0 * inverse_sq)
    far_tensor = 0.75 * (1.0 - 2.0 * inverse_sq) * inverse_sq * inverse
    touching = radius < 2.0
    scalar_part = jnp.where(touching, 1.0 - 9.0 / 32.0 * radius, far_scalar)
    tensor_part = jnp.where(touching, 3.0 / 32.0 * inverse, far_tensor)
    return (separation, scalar_part, tensor_part)


def toward_rows(separation, scalar_part, tensor_part, col_forces):
    projected = jnp.sum(separation * col_forces[:, None, :], axis=0)
    return jnp.sum(
        scalar_part[None] * col_forces[:, None, :] + (tensor_part * projected)[None] * separation,
        axis=2,
    )


def shards(positions, residual, iterate):
    own_blobs = positions.shape[1]
    old_norm = lax.psum(jnp.sum(residual * residual), "tile")
    col_pos = lax.all_gather(positions, "tile", axis=1, tiled=True)
    col_forces = lax.all_gather(residual, "tile", axis=1, tiled=True)
    portion_cols = col_pos.shape[1]
    col_block = portion_cols
    for factor in (4, 2, 1):
        col_block = factor * own_blobs
        break

    def add_block(turn_index, running):
        block_pos = lax.dynamic_slice_in_dim(col_pos, turn_index * col_block, col_block, 1)
        block_forces = lax.dynamic_slice_in_dim(col_forces, turn_index * col_block, col_block, 1)
        separation, scalar_part, tensor_part = pair_terms(positions, block_pos)
        return running + toward_rows(separation, scalar_part, tensor_part, block_forces)

    applied = lax.fori_loop(0, portion_cols // col_block, add_block, jnp.zeros_like(residual))
    curvature = lax.psum(jnp.sum(residual * applied), "tile")
    step_size = old_norm / curvature
    new_residual = residual - step_size * applied
    new_norm = lax.psum(jnp.sum(new_residual * new_residual), "tile")
    new_iterate = iterate + step_size * residual
    new_direction = new_residual + new_norm / old_norm * residual
    return (new_iterate, new_residual, new_direction)


def solution(mesh):
    return jax.shard_map(
        shards,
        mesh=mesh,
        in_specs=(P("real", "tile"), P("real", "tile"), P("real", "tile")),
        out_specs=(P("real", "tile"), P("real", "tile"), P("real", "tile")),
        check_vma=False,
    )
```

profile of v0, /device:TPU:0, one launch (start us, length us, event | category | flops | bytes accessed | tf_op | source)
XLA Modules:
  0.0 165.1 jit_solution(6442482215898881509)
XLA Ops:
  0.6 23.7 %all_gather.6 = f32[3,8192]{1,0:T(4,128)S(1)} all-gather(f32[3,512]{1,0:T(4,128)} %param.5), channel_id=1, replica_groups=mesh['real'=2,'tile'=16] {'tile'}, dimensions={1}, use_global_device_ids=true | all-gather | bytes 104448 | tf_op jit(solution)/shard_map/all_gather | solution.py:32
  24.3 18.0 %all_gather.7 = f32[3,8192]{1,0:T(4,128)S(1)} all-gather(f32[3,512]{1,0:T(4,128)} %param.6), channel_id=1, replica_groups=mesh['real'=2,'tile'=16] {'tile'}, dimensions={1}, use_global_device_ids=true | all-gather | bytes 104448 | tf_op jit(solution)/shard_map/all_gather | solution.py:33
  42.4 56.4 %while.14 = (s32[]{:T(128)}, f32[3,512]{1,0:T(4,128)S(1)}, f32[3,512]{1,0:T(4,128)}, f32[3,8192]{1,0:T(4,128)S(1)}, f32[3,8192]{1,0:T(4,128)S(1)}, /*index=5*/s32[]{:T(128)}, s32[]{:T(128)}, s32[]{:T(128)}, s32[]{:T(128)}) while((s32[]{:T(128)}, f32[3,512]{1,0:T(4,128)S(1)}, f32[3,512]{1,0:T(4,128)}, f32[3,8192]{1,0:T(4,128)S(1)}, ...), condition=%wide.region_6.7_spmd.clone, body=%wide.region_2.6_spmd.clone.sunk | while | flops 49284612 | bytes 33812656 | solution.py:46
  42.4 8.2 %fusion.10 = (f32[512,2048]{1,0:T(8,128)S(1)}, f32[512,2048]{1,0:T(8,128)S(1)}) fusion(f32[3,2048]{1,0:T(4,128)S(1)} %get-tuple-element.177, f32[3,512]{1,0:T(4,128)} %get-tuple-element.203, f32[3,2048]{1,0:T(4,128)S(1)} %get-tuple-element.178), kind=kLoop, calls=%fused_computation.3.clone.1 | loop fusion | flops 13631488 | bytes 8443904 | tf_op jit(solution)/shard_map/while/body/eval_jaxpr/reduce_sum | solution.py:9
  50.6 0.0 copy-start
  50.6 3.6 %fusion.11 = (f32[512,2048]{1,0:T(8,128)S(1)}, f32[512,2048]{1,0:T(8,128)S(1)}) fusion(f32[512,2048]{1,0:T(8,128)S(1)} %get-tuple-element.179, f32[512,2048]{1,0:T(8,128)S(1)} %get-tuple-element.180), kind=kLoop, calls=%fused_computation.11.clone.1 | loop fusion | flops 19922944 | bytes 16777216 | tf_op jit(solution)/shard_map/while/body/eval_jaxpr/jit(_where)/select_n | solution.py:16
  54.2 2.3 %fusion.12 = f32[3,512]{1,0:T(4,128)S(1)} fusion(f32[512,2048]{1,0:T(8,128)S(1)} %get-tuple-element.181, f32[3,2048]{1,0:T(4,128)S(1)} %get-tuple-element.178, f32[512,2048]{1,0:T(8,128)S(1)} %get-tuple-element.182, f32[3,2048]{1,0:T(4,128)S(1)} %get-tuple-element.177, f32[3,512]{1,0:T(4,128)S(1)} %copy-done), kind=kLoop, calls=%fused_computation.6.clone.1 | loop fusion | flops 15727104 | bytes 8450048 | tf_op jit(solution)/shard_map/while/body/eval_jaxpr/reduce_sum | solution.py:23
  56.5 8.2 %fusion.10 = (f32[512,2048]{1,0:T(8,128)S(1)}, f32[512,2048]{1,0:T(8,128)S(1)}) fusion(f32[3,2048]{1,0:T(4,128)S(1)} %get-tuple-element.177, f32[3,512]{1,0:T(4,128)} %get-tuple-element.203, f32[3,2048]{1,0:T(4,128)S(1)} %get-tuple-element.178), kind=kLoop, calls=%fused_computation.3.clone.1 | loop fusion | flops 13631488 | bytes 8443904 | tf_op jit(solution)/shard_map/while/body/eval_jaxpr/reduce_sum | solution.py:9
  64.7 0.0 copy-start
  64.7 3.6 %fusion.11 = (f32[512,2048]{1,0:T(8,128)S(1)}, f32[512,2048]{1,0:T(8,128)S(1)}) fusion(f32[512,2048]{1,0:T(8,128)S(1)} %get-tuple-element.179, f32[512,2048]{1,0:T(8,128)S(1)} %get-tuple-element.180), kind=kLoop, calls=%fused_computation.11.clone.1 | loop fusion | flops 19922944 | bytes 16777216 | tf_op jit(solution)/shard_map/while/body/eval_jaxpr/jit(_where)/select_n | solution.py:16
  68.3 2.3 %fusion.12 = f32[3,512]{1,0:T(4,128)S(1)} fusion(f32[512,2048]{1,0:T(8,128)S(1)} %get-tuple-element.181, f32[3,2048]{1,0:T(4,128)S(1)} %get-tuple-element.178, f32[512,2048]{1,0:T(8,128)S(1)} %get-tuple-element.182, f32[3,2048]{1,0:T(4,128)S(1)} %get-tuple-element.177, f32[3,512]{1,0:T(4,128)S(1)} %copy-done), kind=kLoop, calls=%fused_computation.6.clone.1 | loop fusion | flops 15727104 | bytes 8450048 | tf_op jit(solution)/shard_map/while/body/eval_jaxpr/reduce_sum | solution.py:23
  70.6 8.2 %fusion.10 = (f32[512,2048]{1,0:T(8,128)S(1)}, f32[512,2048]{1,0:T(8,128)S(1)}) fusion(f32[3,2048]{1,0:T(4,128)S(1)} %get-tuple-element.177, f32[3,512]{1,0:T(4,128)} %get-tuple-element.203, f32[3,2048]{1,0:T(4,128)S(1)} %get-tuple-element.178), kind=kLoop, calls=%fused_computation.3.clone.1 | loop fusion | flops 13631488 | bytes 8443904 | tf_op jit(solution)/shard_map/while/body/eval_jaxpr/reduce_sum | solution.py:9
  78.8 0.0 copy-start
  78.8 3.6 %fusion.11 = (f32[512,2048]{1,0:T(8,128)S(1)}, f32[512,2048]{1,0:T(8,128)S(1)}) fusion(f32[512,2048]{1,0:T(8,128)S(1)} %get-tuple-element.179, f32[512,2048]{1,0:T(8,128)S(1)} %get-tuple-element.180), kind=kLoop, calls=%fused_computation.11.clone.1 | loop fusion | flops 19922944 | bytes 16777216 | tf_op jit(solution)/shard_map/while/body/eval_jaxpr/jit(_where)/select_n | solution.py:16
  82.4 2.3 %fusion.12 = f32[3,512]{1,0:T(4,128)S(1)} fusion(f32[512,2048]{1,0:T(8,128)S(1)} %get-tuple-element.181, f32[3,2048]{1,0:T(4,128)S(1)} %get-tuple-element.178, f32[512,2048]{1,0:T(8,128)S(1)} %get-tuple-element.182, f32[3,2048]{1,0:T(4,128)S(1)} %get-tuple-element.177, f32[3,512]{1,0:T(4,128)S(1)} %copy-done), kind=kLoop, calls=%fused_computation.6.clone.1 | loop fusion | flops 15727104 | bytes 8450048 | tf_op jit(solution)/shard_map/while/body/eval_jaxpr/reduce_sum | solution.py:23
  84.7 8.2 %fusion.10 = (f32[512,2048]{1,0:T(8,128)S(1)}, f32[512,2048]{1,0:T(8,128)S(1)}) fusion(f32[3,2048]{1,0:T(4,128)S(1)} %get-tuple-element.177, f32[3,512]{1,0:T(4,128)} %get-tuple-element.203, f32[3,2048]{1,0:T(4,128)S(1)} %get-tuple-element.178), kind=kLoop, calls=%fused_computation.3.clone.1 | loop fusion | flops 13631488 | bytes 8443904 | tf_op jit(solution)/shard_map/while/body/eval_jaxpr/reduce_sum | solution.py:9
  92.9 0.0 copy-start
  92.9 3.6 %fusion.11 = (f32[512,2048]{1,0:T(8,128)S(1)}, f32[512,2048]{1,0:T(8,128)S(1)}) fusion(f32[512,2048]{1,0:T(8,128)S(1)} %get-tuple-element.179, f32[512,2048]{1,0:T(8,128)S(1)} %get-tuple-element.180), kind=kLoop, calls=%fused_computation.11.clone.1 | loop fusion | flops 19922944 | bytes 16777216 | tf_op jit(solution)/shard_map/while/body/eval_jaxpr/jit(_where)/select_n | solution.py:16
  96.5 2.3 %fusion.12 = f32[3,512]{1,0:T(4,128)S(1)} fusion(f32[512,2048]{1,0:T(8,128)S(1)} %get-tuple-element.181, f32[3,2048]{1,0:T(4,128)S(1)} %get-tuple-element.178, f32[512,2048]{1,0:T(8,128)S(1)} %get-tuple-element.182, f32[3,2048]{1,0:T(4,128)S(1)} %get-tuple-element.177, f32[3,512]{1,0:T(4,128)S(1)} %copy-done), kind=kLoop, calls=%fused_computation.6.clone.1 | loop fusion | flops 15727104 | bytes 8450048 | tf_op jit(solution)/shard_map/while/body/eval_jaxpr/reduce_sum | solution.py:23
  98.8 0.6 multiply_reduce_fusion.1
  99.4 31.7 %all-reduce = (f32[]{:T(128)}, f32[]{:T(128)}) all-reduce(f32[]{:T(128)} %get-tuple-element.119, f32[]{:T(128)} %get-tuple-element.118), channel_id=1, replica_groups=mesh['real'=2,'tile'=16] {'tile'}, use_global_device_ids=true, to_apply=%region_1.0 | all-reduce | flops 2 | bytes 16 | tf_op jit(solution)/shard_map/psum | solution.py:31
  132.5 0.6 multiply_reduce_fusion
  133.1 30.1 %psum.23 = f32[]{:T(128)} all-reduce(f32[]{:T(128)} %get-tuple-element.132), channel_id=1, replica_groups=mesh['real'=2,'tile'=16] {'tile'}, use_global_device_ids=true, to_apply=%region_10.11 | all-reduce | flops 1 | bytes 8 | tf_op jit(solution)/shard_map/psum | solution.py:50
  164.5 0.6 multiply_add_fusion
  (19 shorter events, 0.1 us)
Async XLA Ops:
  42.4 56.5 %copy-start.1 = (f32[3,512]{1,0:T(4,128)S(1)}, f32[3,512]{1,0:T(4,128)}, u32[]{:S(2)}) copy-start(f32[3,512]{1,0:T(4,128)} %param.6) | copy-start | bytes 18436
  42.4 122.2 %copy-start.3 = (f32[3,512]{1,0:T(4,128)S(1)}, f32[3,512]{1,0:T(4,128)}, u32[]{:S(2)}) copy-start(f32[3,512]{1,0:T(4,128)} %param.7) | copy-start | bytes 18436
  50.6 3.6 %copy-start = (f32[3,512]{1,0:T(4,128)S(1)}, f32[3,512]{1,0:T(4,128)}, u32[]{:S(2)}) copy-start(f32[3,512]{1,0:T(4,128)} %get-tuple-element.203) | copy-start | bytes 18436 | tf_op jit(solution)/shard_map/while
  64.7 3.6 %copy-start = (f32[3,512]{1,0:T(4,128)S(1)}, f32[3,512]{1,0:T(4,128)}, u32[]{:S(2)}) copy-start(f32[3,512]{1,0:T(4,128)} %get-tuple-element.203) | copy-start | bytes 18436 | tf_op jit(solution)/shard_map/while
  78.8 3.6 %copy-start = (f32[3,512]{1,0:T(4,128)S(1)}, f32[3,512]{1,0:T(4,128)}, u32[]{:S(2)}) copy-start(f32[3,512]{1,0:T(4,128)} %get-tuple-element.203) | copy-start | bytes 18436 | tf_op jit(solution)/shard_map/while
  92.9 3.6 %copy-start = (f32[3,512]{1,0:T(4,128)S(1)}, f32[3,512]{1,0:T(4,128)}, u32[]{:S(2)}) copy-start(f32[3,512]{1,0:T(4,128)} %get-tuple-element.203) | copy-start | bytes 18436 | tf_op jit(solution)/shard_map/while
  133.1 32.1 %copy-start.2 = (f32[3,512]{1,0:T(4,128)}, f32[3,512]{1,0:T(4,128)S(1)}, u32[]{:S(2)}) copy-start(f32[3,512]{1,0:T(4,128)S(1)} %get-tuple-element.133) | copy-start | bytes 18436
where the time goes:
time: 166 us; the launch traced here: 165 us
  blocking collectives  104 us (63%)
  other arithmetic  57.9 us (35%)
  between operations  3.34 us (2%)
    reduce_sum x4, other arithmetic, pair_terms(): squared = jnp.sum(separation * separation, axis=0)  32.7 us
    psum x1, blocking collectives, shards(): old_norm = lax.psum(jnp.sum(residual * residual), 'tile')  31.7 us
    psum x1, blocking collectives, shards(): new_norm = lax.psum(jnp.sum(new_residual * new_residual), 'tile')  30.1 us
    all_gather x1, blocking collectives, shards(): col_pos = lax.all_gather(positions, 'tile', axis=1, tiled=True)  23.7 us
    all_gather x1, blocking collectives, shards(): col_forces = lax.all_gather(residual, 'tile', axis=1, tiled=True)  18 us
    select_n x4, other arithmetic, pair_terms(): scalar_part = jnp.where(touching, 1.0 - 9.0 / 32.0 * radius, far_scalar)  14.3 us
    reduce_sum x4, other arithmetic, toward_rows(): jnp.sum(scalar_part[None] * col_forces[:, None, :] + (tensor_part * proje...  9.06 us

commit v1 on v0

--- a/solution.py
+++ b/solution.py
@@ -30,7 +30,8 @@
     own_blobs = positions.shape[1]
     old_norm = lax.psum(jnp.sum(residual * residual), "tile")
     col_pos = lax.all_gather(positions, "tile", axis=1, tiled=True)
-    col_forces = lax.all_gather(residual, "tile", axis=1, tiled=True)
+    parts = lax.all_gather(residual, "tile")
+    col_forces = jnp.concatenate(parts, axis=1)
     portion_cols = col_pos.shape[1]
     col_block = portion_cols
     for factor in (4, 2, 1):

time: 166 us -> 166 us (level)
  no operation moved by 1% of the time
where the time goes in v1:
time: 166 us; the launch traced here: 165 us
  blocking collectives  104 us (63%)
  other arithmetic  57.9 us (35%)
  between operations  3.34 us (2%)
    reduce_sum x4, other arithmetic, pair_terms(): squared = jnp.sum(separation * separation, axis=0)  32.7 us
    psum x1, blocking collectives, shards(): old_norm = lax.psum(jnp.sum(residual * residual), 'tile')  31.7 us
    psum x1, blocking collectives, shards(): new_norm = lax.psum(jnp.sum(new_residual * new_residual), 'tile')  30.1 us
    all_gather x1, blocking collectives, shards(): col_pos = lax.all_gather(positions, 'tile', axis=1, tiled=True)  23.7 us
    all_gather x1, blocking collectives, shards(): parts = lax.all_gather(residual, 'tile')  18 us
    select_n x4, other arithmetic, pair_terms(): scalar_part = jnp.where(touching, 1.0 - 9.0 / 32.0 * radius, far_scalar)  14.3 us
    reduce_sum x4, other arithmetic, toward_rows(): jnp.sum(scalar_part[None] * col_forces[:, None, :] + (tensor_part * proje...  9.06 us

profile of v1, /device:TPU:0, one launch (start us, length us, event | category | flops | bytes accessed | tf_op | source)
XLA Modules:
  0.0 165.1 jit_solution(10569585680606642884)
XLA Ops:
  0.6 23.7 %all_gather.9 = f32[3,8192]{1,0:T(4,128)S(1)} all-gather(f32[3,512]{1,0:T(4,128)} %param.5), channel_id=1, replica_groups=mesh['real'=2,'tile'=16] {'tile'}, dimensions={1}, use_global_device_ids=true | all-gather | bytes 104448 | tf_op jit(solution)/shard_map/all_gather | solution.py:32
  24.3 18.0 %all-gather.1 = f32[16,3,512]{2,1,0:T(4,128)S(1)} all-gather(f32[1,3,512]{2,1,0:T(4,128)} %bitcast.5), channel_id=2, replica_groups=mesh['real'=2,'tile'=16] {'tile'}, dimensions={0}, use_global_device_ids=true | all-gather | bytes 104448 | tf_op jit(solution)/shard_map/all_gather | solution.py:33
  42.4 56.4 %while.14 = (s32[]{:T(128)}, f32[3,512]{1,0:T(4,128)S(1)}, f32[3,512]{1,0:T(4,128)}, f32[3,8192]{1,0:T(4,128)S(1)}, f32[3,8192]{1,0:T(4,128)S(1)}, /*index=5*/s32[]{:T(128)}, s32[]{:T(128)}, s32[]{:T(128)}, s32[]{:T(128)}) while((s32[]{:T(128)}, f32[3,512]{1,0:T(4,128)S(1)}, f32[3,512]{1,0:T(4,128)}, f32[3,8192]{1,0:T(4,128)S(1)}, ...), condition=%wide.region_6.7_spmd.clone, body=%wide.region_2.6_spmd.clone.sunk | while | flops 49284612 | bytes 33812656 | solution.py:47
  42.4 8.2 %fusion.10 = (f32[512,2048]{1,0:T(8,128)S(1)}, f32[512,2048]{1,0:T(8,128)S(1)}) fusion(f32[3,2048]{1,0:T(4,128)S(1)} %get-tuple-element.177, f32[3,512]{1,0:T(4,128)} %get-tuple-element.203, f32[3,2048]{1,0:T(4,128)S(1)} %get-tuple-element.178), kind=kLoop, calls=%fused_computation.3.clone.1 | loop fusion | flops 13631488 | bytes 8443904 | tf_op jit(solution)/shard_map/while/body/eval_jaxpr/reduce_sum | solution.py:9
  50.6 0.0 copy-start
  50.6 3.6 %fusion.11 = (f32[512,2048]{1,0:T(8,128)S(1)}, f32[512,2048]{1,0:T(8,128)S(1)}) fusion(f32[512,2048]{1,0:T(8,128)S(1)} %get-tuple-element.179, f32[512,2048]{1,0:T(8,128)S(1)} %get-tuple-element.180), kind=kLoop, calls=%fused_computation.11.clone.1 | loop fusion | flops 19922944 | bytes 16777216 | tf_op jit(solution)/shard_map/while/body/eval_jaxpr/jit(_where)/select_n | solution.py:16
  54.2 2.3 %fusion.12 = f32[3,512]{1,0:T(4,128)S(1)} fusion(f32[512,2048]{1,0:T(8,128)S(1)} %get-tuple-element.181, f32[3,2048]{1,0:T(4,128)S(1)} %get-tuple-element.178, f32[512,2048]{1,0:T(8,128)S(1)} %get-tuple-element.182, f32[3,2048]{1,0:T(4,128)S(1)} %get-tuple-element.177, f32[3,512]{1,0:T(4,128)S(1)} %copy-done), kind=kLoop, calls=%fused_computation.6.clone.1 | loop fusion | flops 15727104 | bytes 8450048 | tf_op jit(solution)/shard_map/while/body/eval_jaxpr/reduce_sum | solution.py:23
  56.5 8.2 %fusion.10 = (f32[512,2048]{1,0:T(8,128)S(1)}, f32[512,2048]{1,0:T(8,128)S(1)}) fusion(f32[3,2048]{1,0:T(4,128)S(1)} %get-tuple-element.177, f32[3,512]{1,0:T(4,128)} %get-tuple-element.203, f32[3,2048]{1,0:T(4,128)S(1)} %get-tuple-element.178), kind=kLoop, calls=%fused_computation.3.clone.1 | loop fusion | flops 13631488 | bytes 8443904 | tf_op jit(solution)/shard_map/while/body/eval_jaxpr/reduce_sum | solution.py:9
  64.7 0.0 copy-start
  64.7 3.6 %fusion.11 = (f32[512,2048]{1,0:T(8,128)S(1)}, f32[512,2048]{1,0:T(8,128)S(1)}) fusion(f32[512,2048]{1,0:T(8,128)S(1)} %get-tuple-element.179, f32[512,2048]{1,0:T(8,128)S(1)} %get-tuple-element.180), kind=kLoop, calls=%fused_computation.11.clone.1 | loop fusion | flops 19922944 | bytes 16777216 | tf_op jit(solution)/shard_map/while/body/eval_jaxpr/jit(_where)/select_n | solution.py:16
  68.3 2.3 %fusion.12 = f32[3,512]{1,0:T(4,128)S(1)} fusion(f32[512,2048]{1,0:T(8,128)S(1)} %get-tuple-element.181, f32[3,2048]{1,0:T(4,128)S(1)} %get-tuple-element.178, f32[512,2048]{1,0:T(8,128)S(1)} %get-tuple-element.182, f32[3,2048]{1,0:T(4,128)S(1)} %get-tuple-element.177, f32[3,512]{1,0:T(4,128)S(1)} %copy-done), kind=kLoop, calls=%fused_computation.6.clone.1 | loop fusion | flops 15727104 | bytes 8450048 | tf_op jit(solution)/shard_map/while/body/eval_jaxpr/reduce_sum | solution.py:23
  70.6 8.2 %fusion.10 = (f32[512,2048]{1,0:T(8,128)S(1)}, f32[512,2048]{1,0:T(8,128)S(1)}) fusion(f32[3,2048]{1,0:T(4,128)S(1)} %get-tuple-element.177, f32[3,512]{1,0:T(4,128)} %get-tuple-element.203, f32[3,2048]{1,0:T(4,128)S(1)} %get-tuple-element.178), kind=kLoop, calls=%fused_computation.3.clone.1 | loop fusion | flops 13631488 | bytes 8443904 | tf_op jit(solution)/shard_map/while/body/eval_jaxpr/reduce_sum | solution.py:9
  78.8 0.0 copy-start
  78.8 3.6 %fusion.11 = (f32[512,2048]{1,0:T(8,128)S(1)}, f32[512,2048]{1,0:T(8,128)S(1)}) fusion(f32[512,2048]{1,0:T(8,128)S(1)} %get-tuple-element.179, f32[512,2048]{1,0:T(8,128)S(1)} %get-tuple-element.180), kind=kLoop, calls=%fused_computation.11.clone.1 | loop fusion | flops 19922944 | bytes 16777216 | tf_op jit(solution)/shard_map/while/body/eval_jaxpr/jit(_where)/select_n | solution.py:16
  82.4 2.3 %fusion.12 = f32[3,512]{1,0:T(4,128)S(1)} fusion(f32[512,2048]{1,0:T(8,128)S(1)} %get-tuple-element.181, f32[3,2048]{1,0:T(4,128)S(1)} %get-tuple-element.178, f32[512,2048]{1,0:T(8,128)S(1)} %get-tuple-element.182, f32[3,2048]{1,0:T(4,128)S(1)} %get-tuple-element.177, f32[3,512]{1,0:T(4,128)S(1)} %copy-done), kind=kLoop, calls=%fused_computation.6.clone.1 | loop fusion | flops 15727104 | bytes 8450048 | tf_op jit(solution)/shard_map/while/body/eval_jaxpr/reduce_sum | solution.py:23
  84.7 8.2 %fusion.10 = (f32[512,2048]{1,0:T(8,128)S(1)}, f32[512,2048]{1,0:T(8,128)S(1)}) fusion(f32[3,2048]{1,0:T(4,128)S(1)} %get-tuple-element.177, f32[3,512]{1,0:T(4,128)} %get-tuple-element.203, f32[3,2048]{1,0:T(4,128)S(1)} %get-tuple-element.178), kind=kLoop, calls=%fused_computation.3.clone.1 | loop fusion | flops 13631488 | bytes 8443904 | tf_op jit(solution)/shard_map/while/body/eval_jaxpr/reduce_sum | solution.py:9
  92.9 0.0 copy-start
  92.9 3.6 %fusion.11 = (f32[512,2048]{1,0:T(8,128)S(1)}, f32[512,2048]{1,0:T(8,128)S(1)}) fusion(f32[512,2048]{1,0:T(8,128)S(1)} %get-tuple-element.179, f32[512,2048]{1,0:T(8,128)S(1)} %get-tuple-element.180), kind=kLoop, calls=%fused_computation.11.clone.1 | loop fusion | flops 19922944 | bytes 16777216 | tf_op jit(solution)/shard_map/while/body/eval_jaxpr/jit(_where)/select_n | solution.py:16
  96.5 2.3 %fusion.12 = f32[3,512]{1,0:T(4,128)S(1)} fusion(f32[512,2048]{1,0:T(8,128)S(1)} %get-tuple-element.181, f32[3,2048]{1,0:T(4,128)S(1)} %get-tuple-element.178, f32[512,2048]{1,0:T(8,128)S(1)} %get-tuple-element.182, f32[3,2048]{1,0:T(4,128)S(1)} %get-tuple-element.177, f32[3,512]{1,0:T(4,128)S(1)} %copy-done), kind=kLoop, calls=%fused_computation.6.clone.1 | loop fusion | flops 15727104 | bytes 8450048 | tf_op jit(solution)/shard_map/while/body/eval_jaxpr/reduce_sum | solution.py:23
  98.8 0.6 multiply_reduce_fusion.1
  99.4 31.7 %all-reduce = (f32[]{:T(128)}, f32[]{:T(128)}) all-reduce(f32[]{:T(128)} %get-tuple-element.119, f32[]{:T(128)} %get-tuple-element.118), channel_id=1, replica_groups=mesh['real'=2,'tile'=16] {'tile'}, use_global_device_ids=true, to_apply=%region_1.0 | all-reduce | flops 2 | bytes 16 | tf_op jit(solution)/shard_map/psum | solution.py:31
  132.5 0.6 multiply_reduce_fusion
  133.1 30.1 %psum.23 = f32[]{:T(128)} all-reduce(f32[]{:T(128)} %get-tuple-element.132), channel_id=1, replica_groups=mesh['real'=2,'tile'=16] {'tile'}, use_global_device_ids=true, to_apply=%region_10.11 | all-reduce | flops 1 | bytes 8 | tf_op jit(solution)/shard_map/psum | solution.py:51
  164.5 0.6 multiply_add_fusion
  (19 shorter events, 0.1 us)
Async XLA Ops:
  42.4 56.5 %copy-start.1 = (f32[3,512]{1,0:T(4,128)S(1)}, f32[3,512]{1,0:T(4,128)}, u32[]{:S(2)}) copy-start(f32[3,512]{1,0:T(4,128)} %param.6) | copy-start | bytes 18436
  42.4 122.2 %copy-start.3 = (f32[3,512]{1,0:T(4,128)S(1)}, f32[3,512]{1,0:T(4,128)}, u32[]{:S(2)}) copy-start(f32[3,512]{1,0:T(4,128)} %param.7) | copy-start | bytes 18436
  50.6 3.6 %copy-start = (f32[3,512]{1,0:T(4,128)S(1)}, f32[3,512]{1,0:T(4,128)}, u32[]{:S(2)}) copy-start(f32[3,512]{1,0:T(4,128)} %get-tuple-element.203) | copy-start | bytes 18436 | tf_op jit(solution)/shard_map/while
  64.7 3.6 %copy-start = (f32[3,512]{1,0:T(4,128)S(1)}, f32[3,512]{1,0:T(4,128)}, u32[]{:S(2)}) copy-start(f32[3,512]{1,0:T(4,128)} %get-tuple-element.203) | copy-start | bytes 18436 | tf_op jit(solution)/shard_map/while
  78.8 3.6 %copy-start = (f32[3,512]{1,0:T(4,128)S(1)}, f32[3,512]{1,0:T(4,128)}, u32[]{:S(2)}) copy-start(f32[3,512]{1,0:T(4,128)} %get-tuple-element.203) | copy-start | bytes 18436 | tf_op jit(solution)/shard_map/while
  92.9 3.6 %copy-start = (f32[3,512]{1,0:T(4,128)S(1)}, f32[3,512]{1,0:T(4,128)}, u32[]{:S(2)}) copy-start(f32[3,512]{1,0:T(4,128)} %get-tuple-element.203) | copy-start | bytes 18436 | tf_op jit(solution)/shard_map/while
  133.1 32.1 %copy-start.2 = (f32[3,512]{1,0:T(4,128)}, f32[3,512]{1,0:T(4,128)S(1)}, u32[]{:S(2)}) copy-start(f32[3,512]{1,0:T(4,128)S(1)} %get-tuple-element.133) | copy-start | bytes 18436
